TPU v7x, 128 devices: a whole 4x4x4 slice. The times are simulated.
128 devices in a mesh: dst: 32 (over y, x, core), src: 4 (over z).
Axes of the slice: x: 4, y: 4, z: 4, core: 2. Of those that a mesh axis runs over, the one named last changes fastest.
Arguments:
- points: bfloat16 [16384, 256], P(('dst', 'src')), may hold values from -6 to 6
- w_query: bfloat16 [256, 256], replicated, may hold values from -16 to 16
- w_key: bfloat16 [256, 256], replicated, may hold values from -0.375 to 0.375
- w_value: bfloat16 [256, 256], replicated, may hold values from -0.375 to 0.375
- w_out: bfloat16 [256, 256], replicated, may hold values from -0.375 to 0.375
- gain: float32 [256], replicated, may hold values from 0.25 to 1.75
- cell_counts: int32 [32, 4], P('dst', 'src'), may hold values from 8 to 64, as said below
- tile_slots: int32 [32, 4, 64], P('dst', 'src'), may hold values from 0 to 127, as said below
- edge_masks: int32 [32, 4, 64, 128, 128], P('dst', 'src'), may hold values 0 or 1
Outputs:
- out_points: bfloat16 [16384, 256], P(('dst', 'src'))
Inputs may be any that keep to these rules, and one draw needn't show every extreme that they name: `cell_counts`: the busiest cell lists exactly 64 tiles. `tile_slots`: within one cell the 64 tile numbers are all different.
All inputs are finite; a program needn't handle non-finite values. No bound on the sum of `edge_masks` on one device may be relied on, other than what follows from the above.
Results may differ from a plain program's by a relative error of at most 0.0085.
The roundings to bfloat16 on the way count: a program that leaves them out, or rounds other values in their place, can miss the bound.
Values may be sent and summed in bfloat16 or wider, within the bound.
No kernel may reach another device: no remote copies, remote signals or barrier semaphores. Data moves between devices by JAX's collectives and lax.ppermute only.
A program may use at most 64 MiB of HBM per device.

v0:
```python
import functools

import jax
import jax.numpy as jnp
from jax import lax
from jax.experimental import pallas as pl
from jax.experimental.pallas import tpu as pltpu
from jax.sharding import PartitionSpec as P


HEADS = 4
TILE = 128
PAIR = 2 * TILE
VROWS = TILE + 16
MASKED = -1e30
FLOOR = -1e29
PREP = 8
QUAD = 4
OCT = 8
STRIDE = 40
F32 = jnp.float32
BF16 = jnp.bfloat16
VM = pltpu.VMEM
SM = pltpu.SMEM


def inverse_sinh(ratio):
    return jnp.log(ratio + jnp.sqrt(ratio * ratio + 1.0))


def tangent_kernel(points_ref, out_ref):
    values = points_ref[...].astype(F32)
    radius = jnp.sqrt(jnp.sum(values * values, axis=-1, keepdims=True) + 1e-06)
    ratio = radius / 16.0
    out_ref[...] = (16.0 * inverse_sinh(ratio) * values / radius).astype(BF16)


def log_map(points):
    vm = pl.BlockSpec(memory_space=VM)
    return pl.pallas_call(
        tangent_kernel,
        in_specs=[vm],
        out_specs=vm,
        out_shape=jax.ShapeDtypeStruct(points.shape, BF16),
        compiler_params=pltpu.CompilerParams(vmem_limit_bytes=2 << 20),
        cost_estimate=pl.CostEstimate(flops=1 << 18, bytes_accessed=1 << 17, transcendentals=1 << 9),
        name="tangent",
    )(points)


def gray(delta):
    return delta ^ (delta >> 1)


def prep_kernel(live_ref, codes, mask_hbm, bias_hbm, tile_out, count_out, mask_ref, bias_ref, sem, out_sem):
    spare = mask_hbm.shape[0]
    live = live_ref[0]

    def fetch(trip):
        span = pl.ds(trip * PREP, PREP)
        return pltpu.make_async_copy(mask_hbm.at[span], mask_ref.at[span], sem.at[trip])

    def store(trip):
        span = pl.ds(trip * PREP, PREP)
        return pltpu.make_async_copy(bias_ref.at[span], bias_hbm.at[span], out_sem.at[trip])

    last = pltpu.make_async_copy(bias_ref.at[pl.ds(spare, 1)], bias_hbm.at[pl.ds(spare, 1)], out_sem.at[spare // PREP])
    for trip in range(spare // PREP):
        fetch(trip).start()
    row = lax.broadcasted_iota(jnp.int32, (TILE, TILE), 0)
    lane = lax.broadcasted_iota(jnp.int32, (TILE, TILE), 1)
    eye = jnp.where(row == lane, 1.0, 0.0).astype(BF16)
    bias_ref[spare] = jnp.full((TILE, TILE), MASKED, BF16)
    last.start()
    for group in range(4):
        count_out[group] = 0

    def step(trip, _):
        fetch(trip).wait()
        for member in range(PREP):
            slot = trip * PREP + member
            group = codes[slot]
            is_live = slot < live
            at = count_out[group]
            tile_out[jnp.where(is_live, group * STRIDE + at, 4 * STRIDE)] = slot
            count_out[group] = jnp.where(is_live, at + 1, at)
            wanted = jnp.where(is_live, 1, 2)
            bias = jnp.where(mask_ref[slot] == wanted, 0.0, MASKED).astype(BF16)
            bias_ref[slot] = nt_dot(eye, bias).astype(BF16)
        store(trip).start()
        return 0

    lax.fori_loop(0, spare // PREP, step, 0)
    for group in range(4):
        for extra in range(QUAD):
            tile_out[group * STRIDE + count_out[group] + extra] = spare
    for trip in range(spare // PREP):
        store(trip).wait()
    last.wait()


def prepare(live, codes, masks):
    tiles = masks.shape[0]
    vm = pl.BlockSpec(memory_space=VM)
    sm = pl.BlockSpec(memory_space=SM)
    return pl.pallas_call(
        prep_kernel,
        in_specs=[sm, sm, pl.BlockSpec(memory_space=pltpu.HBM)],
        out_specs=[pl.BlockSpec(memory_space=pltpu.HBM), sm, sm],
        out_shape=[
            jax.ShapeDtypeStruct((tiles + 1, TILE, TILE), BF16),
            jax.ShapeDtypeStruct((4 * STRIDE + 8,), jnp.int32),
            jax.ShapeDtypeStruct((4,), jnp.int32),
        ],
        scratch_shapes=[
            VM(masks.shape, jnp.int32),
            VM((tiles + 1, TILE, TILE), BF16),
            pltpu.SemaphoreType.DMA((tiles // PREP,)),
            pltpu.SemaphoreType.DMA((tiles // PREP + 1,)),
        ],
        compiler_params=pltpu.CompilerParams(vmem_limit_bytes=61000000),
        cost_estimate=pl.CostEstimate(flops=1 << 20, bytes_accessed=6 << 20, transcendentals=0),
        name="prep",
    )(live, codes, masks)


def nt_dot(left, right):
    return lax.dot_general(left, right, (((1,), (1,)), ((), ())), preferred_element_type=F32)


def project_rows(first_ref, second_ref, wk, wv, key_ref, value_ref, base):
    ones = jnp.ones((VROWS - TILE, TILE), BF16)

    @pl.loop(0, 4, unroll=True)
    def _(step):
        rows = []
        turned = (step & 1) * 2 + (step >> 1)
        for member in range(4):
            rows.append(first_ref[pl.ds(pl.multiple_of((step * 4 + member) * 64, 64), 64), :])
            rows.append(second_ref[pl.ds(pl.multiple_of((turned * 4 + member) * 64, 64), 64), :])
        rows = jnp.concatenate(rows, axis=0)
        keys = jnp.dot(rows, wk, preferred_element_type=F32).astype(BF16)
        values = nt_dot(wv, rows).astype(BF16)
        for member in range(4):
            at = base + step * 4 + member
            span = slice(member * TILE, (member + 1) * TILE)
            key_ref[at] = keys[span]
            for half in range(2):
                value_ref[at, half, pl.ds(0, TILE), :] = values[half * TILE : (half + 1) * TILE, span]
                value_ref[at, half, pl.ds(TILE, VROWS - TILE), :] = ones


def project_kernel(
    first_ref, second_ref, block_ref, wq_ref, wk_ref, wv_ref, key_ref, value_ref, query_ref, turned_ref, own_ref, self_ref
):
    wq, wk = wq_ref[...], wk_ref[...]
    wv_t = wv_ref[...].astype(F32).T.astype(BF16)
    turned_ref[...] = wv_t
    wq_t = wq.astype(F32).T.astype(BF16)
    zero = jnp.zeros((64, TILE), BF16)
    for group in range(4):
        qt = nt_dot(wq_t, block_ref[group]).astype(BF16).astype(F32) * 0.125
        low = qt.astype(BF16)
        for half in range(2):
            upper = jnp.concatenate([low[half * TILE : half * TILE + 64], zero], axis=1)
            lower = jnp.concatenate([zero, low[half * TILE + 64 : half * TILE + TILE]], axis=1)
            query_ref[group, half] = jnp.concatenate([upper, lower], axis=0)
        if group == 0:
            wk_t = wk.astype(F32).T.astype(BF16)
            product = qt * nt_dot(wk_t, block_ref[0]).astype(BF16).astype(F32)
            for head in range(HEADS):
                total = jnp.sum(product[head * 64 : (head + 1) * 64], axis=0, keepdims=True)
                self_ref[pl.ds(head, 1), :] = total
            own_ref[...] = nt_dot(wv_t, block_ref[0]).astype(BF16)
    project_rows(first_ref, second_ref, wk, wv_t, key_ref, value_ref, 0)


def project(first, second, block, w_query, w_key, w_value):
    vm = pl.BlockSpec(memory_space=VM)
    return pl.pallas_call(
        project_kernel,
        in_specs=[vm] * 6,
        out_specs=[vm] * 6,
        out_shape=[
            jax.ShapeDtypeStruct((16, TILE, 256), BF16),
            jax.ShapeDtypeStruct((16, 2, VROWS, TILE), BF16),
            jax.ShapeDtypeStruct((4, 2, TILE, PAIR), BF16),
            jax.ShapeDtypeStruct((256, 256), BF16),
            jax.ShapeDtypeStruct((256, TILE), BF16),
            jax.ShapeDtypeStruct((HEADS, TILE), F32),
        ],
        compiler_params=pltpu.CompilerParams(vmem_limit_bytes=8 << 20),
        cost_estimate=pl.CostEstimate(flops=1 << 29, bytes_accessed=4 << 20, transcendentals=0),
        name="project",
    )(first, second, block, w_query, w_key, w_value)


def attend_rows(
    group, spot_list, tile_list, counts, bias_ref, query_ref, key_ref, value_ref, part_ref, acc_ref, score_ref
):
    base = group * STRIDE
    count = counts[group]
    most = count // OCT
    quads = (count - most * OCT + 1) // QUAD
    quad_at = most * OCT
    rest_at = quad_at + quads * QUAD
    rest = (count - rest_at + 1) // 2

    def score(start, size, tops):
        tops = list(tops)
        names = [tile_list[base + start + member] for member in range(size)]
        spots = [spot_list[name] for name in names]
        for half in range(2):
            keys = jnp.concatenate([key_ref[spot, :, half * TILE : (half + 1) * TILE] for spot in spots], axis=0)
            scores = jnp.dot(keys, query_ref[group, half], preferred_element_type=F32)
            for member in range(size):
                bias = bias_ref[names[member]].astype(F32)
                part = scores[member * TILE : (member + 1) * TILE] + jnp.concatenate([bias, bias], axis=1)
                score_ref[start + member, half] = part
                tops[half] = jnp.maximum(tops[half], jnp.max(part.reshape(16, 8, PAIR), axis=0))
        return tuple(tops)

    floor = jnp.full((8, PAIR), FLOOR, F32)
    tops = lax.fori_loop(0, most, lambda trip, tops: score(trip * OCT, OCT, tops), (floor, floor))
    tops = lax.fori_loop(0, quads, lambda trip, tops: score(quad_at + trip * QUAD, QUAD, tops), tops)
    tops = lax.fori_loop(0, rest, lambda trip, tops: score(rest_at + trip * 2, 2, tops), tops)
    tops = [jnp.max(top, axis=0, keepdims=True) for top in tops]
    acc_ref[...] = jnp.zeros(acc_ref.shape, F32)

    def mix(start, size):
        spots = [spot_list[tile_list[base + start + member]] for member in range(size)]
        for half in range(2):
            weights = [jnp.exp(score_ref[start + member, half] - tops[half]).astype(BF16) for member in range(size)]
            values = jnp.concatenate([value_ref[spot, half] for spot in spots], axis=1)
            acc_ref[half] += jnp.dot(values, jnp.concatenate(weights, axis=0), preferred_element_type=F32)
        return 0

    lax.fori_loop(0, most, lambda trip, _: mix(trip * OCT, OCT), 0)
    lax.fori_loop(0, quads, lambda trip, _: mix(quad_at + trip * QUAD, QUAD), 0)
    lax.fori_loop(0, rest, lambda trip, _: mix(rest_at + trip * 2, 2), 0)
    for half in range(2):
        acc = acc_ref[half]
        part_ref[pl.ds(half * TILE, 64), :] = acc[:64, :TILE].astype(BF16)
        part_ref[pl.ds(half * TILE + 64, 64), :] = acc[64:TILE, TILE:].astype(BF16)
    spans = [(head // 2, slice((head % 2) * TILE, (head % 2 + 1) * TILE)) for head in range(HEADS)]
    rows = [tops[half][:, lanes] for half, lanes in spans]
    rows += [acc_ref[half, pl.ds(TILE, 1), lanes] for half, lanes in spans]
    left = jnp.concatenate(rows, axis=0)
    pieces = []
    for _ in range(4):
        piece = left.astype(BF16)
        pieces.append(piece)
        left = left - piece.astype(F32)
    part_ref[pl.ds(256, 32), :] = jnp.concatenate(pieces, axis=0)


def join_kernel(first_ref, second_ref, wk_ref, wv_ref, near_keys, near_values, key_ref, value_ref, sem):
    copies = [
        pltpu.make_async_copy(near_keys, key_ref.at[pl.ds(0, 16)], sem.at[0]),
        pltpu.make_async_copy(near_values, value_ref.at[pl.ds(0, 16)], sem.at[1]),
    ]
    for copy in copies:
        copy.start()
    project_rows(first_ref, second_ref, wk_ref[...], wv_ref[...], key_ref, value_ref, 16)
    for copy in copies:
        copy.wait()


def join(first, second, w_key, wv_t, keys, values):
    vm = pl.BlockSpec(memory_space=VM)
    return pl.pallas_call(
        join_kernel,
        in_specs=[vm] * 6,
        out_specs=[vm] * 2,
        out_shape=[
            jax.ShapeDtypeStruct((32, TILE, 256), BF16),
            jax.ShapeDtypeStruct((32, 2, VROWS, TILE), BF16),
        ],
        scratch_shapes=[pltpu.SemaphoreType.DMA((2,))],
        compiler_params=pltpu.CompilerParams(vmem_limit_bytes=4 << 20),
        cost_estimate=pl.CostEstimate(flops=1 << 29, bytes_accessed=4 << 20, transcendentals=0),
        name="join",
    )(first, second, w_key, wv_t, keys, values)


def attend(group, lists, bias, queries, keys, values):
    vm = pl.BlockSpec(memory_space=VM)
    sm = pl.BlockSpec(memory_space=SM)
    return pl.pallas_call(
        functools.partial(attend_rows, group),
        in_specs=[sm] * 3 + [vm] * 4,
        out_specs=vm,
        out_shape=jax.ShapeDtypeStruct((288, TILE), BF16),
        scratch_shapes=[VM((2, VROWS, PAIR), F32), VM((36, 2, TILE, PAIR), F32)],
        compiler_params=pltpu.CompilerParams(vmem_limit_bytes=14 << 20),
        cost_estimate=pl.CostEstimate(flops=1 << 30, bytes_accessed=8 << 20, transcendentals=1 << 20),
    )(*lists, bias, queries, keys, values)


def finish_kernel(part0, part1, part2, part3, tangent_ref, own_ref, self_ref, wo_ref, gain_ref, out_ref):
    parts = (part0, part1, part2, part3)
    tangent = tangent_ref[...]
    vt = own_ref[...].astype(F32)
    stats = []
    for cell in range(4):
        pieces = parts[cell][pl.ds(256, 32), :].astype(F32)
        stats.append(pieces[:8] + pieces[8:16] + pieces[16:24] + pieces[24:])
    mixed = []
    for head in range(HEADS):
        rows = slice(head * 64, head * 64 + 64)
        own = self_ref[pl.ds(head, 1), :]
        tops = [stat[head : head + 1] for stat in stats]
        top = own
        for other in tops:
            top = jnp.maximum(top, other)
        own_exp = jnp.exp(own - top)
        total = own_exp
        weighted = own_exp.astype(BF16).astype(F32) * vt[rows]
        for cell in range(4):
            factor = jnp.exp(tops[cell] - top)
            total += stats[cell][4 + head : 5 + head] * factor
            weighted += parts[cell][pl.ds(head * 64, 64), :].astype(F32) * factor
        mixed.append((weighted / total).astype(BF16))
    mixed = jnp.concatenate(mixed, axis=0)
    shifted = tangent.astype(F32) + lax.dot_general(
        mixed, wo_ref[...], (((0,), (0,)), ((), ())), preferred_element_type=F32
    )
    normed = shifted / jnp.sqrt(jnp.mean(shifted * shifted, axis=-1, keepdims=True) + 1e-06) * gain_ref[...]
    radius = jnp.sqrt(jnp.sum(normed * normed, axis=-1, keepdims=True) + 1e-06)
    ratio = radius / 16.0
    square = ratio * ratio
    series = ratio * (
        1.0 + square / 6.0 * (1.0 + square / 20.0 * (1.0 + square / 42.0 * (1.0 + square / 72.0)))
    )
    plain = 0.5 * (jnp.exp(ratio) - jnp.exp(-ratio))
    stretched = jnp.where(ratio < 0.75, series, plain)
    out_ref[...] = (16.0 * stretched * normed / radius).astype(BF16)


def finish(parts, tangent, own, self_score, w_out, gain):
    vm = pl.BlockSpec(memory_space=VM)
    return pl.pallas_call(
        finish_kernel,
        in_specs=[vm] * 9,
        out_specs=vm,
        out_shape=jax.ShapeDtypeStruct(tangent.shape, BF16),
        compiler_params=pltpu.CompilerParams(vmem_limit_bytes=8 << 20),
        cost_estimate=pl.CostEstimate(flops=1 << 26, bytes_accessed=1 << 20, transcendentals=1 << 12),
        name="finish",
    )(*parts, tangent, own, self_score, w_out, gain)


def swap(value, axis, size, mask):
    return lax.ppermute(value, axis, [(at, at ^ mask) for at in range(size)])


def grow(value, axis, size, mask):
    return jnp.concatenate([value, swap(value, axis, size, mask)], axis=0)


def per_device(points, w_query, w_key, w_value, w_out, gain, cell_counts, tile_slots, edge_masks):
    me_dst = lax.axis_index("dst")
    me_src = lax.axis_index("src")
    named = tile_slots[0, 0]
    codes = gray((named >> 5) ^ me_src)
    delta = (named & 31) ^ me_dst
    along_x, along_y = gray((delta >> 1) & 3), gray((delta >> 3) & 3)
    spots = (delta & 1) * 16 + (along_y >> 1) * 8 + (along_x >> 1) * 4 + (along_y & 1) * 2 + (along_x & 1)
    spots = jnp.concatenate([spots, jnp.zeros((8,), jnp.int32)])
    tangent = log_map(points)
    near = swap(tangent, "dst", 32, 2)
    block = grow(tangent, "src", 4, 1)
    near = jnp.concatenate([tangent[:64], near[:64], tangent[64:], near[64:]], axis=0)
    next_near = swap(near, "dst", 32, 8)
    block = grow(block, "src", 4, 3)
    first = jnp.concatenate([near[:128], next_near[:128]], axis=0)
    second = jnp.concatenate([near[128:], next_near[128:]], axis=0)
    first, second = lax.optimization_barrier((first, second))
    for (one, other) in ((6, 24), (24, 6)):
        new_first = grow(first, "dst", 32, one)
        second = grow(second, "dst", 32, other)
        first = new_first
    far_first = swap(first, "dst", 32, 1)
    far_second = swap(second, "dst", 32, 1)
    bias, *lists = prepare(cell_counts[0], codes, edge_masks[0, 0])
    keys, values, queries, wv_t, own, self_score = project(
        first, second, block.reshape(4, TILE, 256), w_query, w_key, w_value
    )
    keys, values = join(far_first, far_second, w_key, wv_t, keys, values)
    parts = []
    for group, mask in ((3, 2), (2, 3), (1, 1), (0, 0)):
        part = attend(group, (spots, *lists), bias, queries, keys, values)
        if group:
            part = swap(part, "src", 4, mask)
        parts.append(part)
    return finish(parts, tangent, own, self_score, w_out, gain[None, :])


def solution(mesh):
    return jax.shard_map(
        per_device,
        mesh=mesh,
        in_specs=(
            P(("dst", "src"), None),
            P(),
            P(),
            P(),
            P(),
            P(),
            P("dst", "src"),
            P("dst", "src", None),
            P("dst", "src", None, None, None),
        ),
        out_specs=P(("dst", "src"), None),
        check_vma=False,
    )
```

profile of v0, /device:TPU:1, one launch (start us, length us, event | category | flops | bytes accessed | tf_op | source)
XLA Modules:
  0.0 60.6 jit_solution(11561996445588600783)
XLA Ops:
  0.0 0.0 copy-start.3
  0.0 0.8 %copy-done.3 = bf16[128,256]{1,0:T(8,128)(2,1)S(1)} copy-done((bf16[128,256]{1,0:T(8,128)(2,1)S(1)}, bf16[128,256]{1,0:T(8,128)(2,1)}, u32[]{:S(2)}) %copy-start.3) | copy-done | bytes 65560
  0.8 0.2 tangent.1.tangent_ref
  1.0 2.1 %collective-permute-start = (bf16[128,256]{1,0:T(8,128)(2,1)S(1)}, bf16[128,256]{1,0:T(8,128)(2,1)S(1)}, u32[]{:S(2)}, u32[]{:S(2)}) collective-permute-start(bf16[128,256]{1,0:T(8,128)(2,1)S(1)} %tangent.1.tangent_ref), channel_id=1, source_target_pairs={{0,8},{4,12},{8,0},{12,4},{16,24},{20,28},{24,16},{28,20},{32,40},... | collective-permute-start | bytes 196616 | tf_op jit(solution)/shard_map/ppermute | solution.py:354
  3.1 1.6 %collective-permute-done = bf16[128,256]{1,0:T(8,128)(2,1)S(1)} collective-permute-done((bf16[128,256]{1,0:T(8,128)(2,1)S(1)}, bf16[128,256]{1,0:T(8,128)(2,1)S(1)}, u32[]{:S(2)}, u32[]{:S(2)}) %collective-permute-start) | collective-permute-done | bytes 65568 | tf_op jit(solution)/shard_map/ppermute | solution.py:354
  4.8 0.0 copy-start.9
  4.8 1.6 %collective-permute-start.1 = (bf16[256,256]{1,0:T(8,128)(2,1)S(1)}, bf16[256,256]{1,0:T(8,128)(2,1)S(1)}, u32[]{:S(2)}, u32[]{:S(2)}) collective-permute-start(bf16[256,256]{1,0:T(8,128)(2,1)S(1)} %pad_maximum_fusion.3), channel_id=1, source_target_pairs={{0,32},{4,36},{8,40},{12,44},{16,48},{20,52},{24,56},{28,60},{32,0... | collective-permute-start | bytes 393224 | tf_op jit(solution)/shard_map/ppermute | solution.py:354
  6.4 1.6 %collective-permute-start.6 = (bf16[128,256]{1,0:T(8,128)(2,1)S(1)}, bf16[128,256]{1,0:T(8,128)(2,1)S(1)}, u32[]{:S(2)}, u32[]{:S(2)}) collective-permute-start(bf16[128,256]{1,0:T(8,128)(2,1)S(1)} %tangent.1.tangent_ref), channel_id=1, source_target_pairs={{0,1},{1,0},{2,3},{3,2},{4,5},{5,4},{6,7},{7,6},{8,9},{9,8},{10,11... | collective-permute-start | bytes 196616 | tf_op jit(solution)/shard_map/ppermute | solution.py:354
  8.1 0.7 %collective-permute-done.1 = bf16[256,256]{1,0:T(8,128)(2,1)S(1)} collective-permute-done((bf16[256,256]{1,0:T(8,128)(2,1)S(1)}, bf16[256,256]{1,0:T(8,128)(2,1)S(1)}, u32[]{:S(2)}, u32[]{:S(2)}) %collective-permute-start.1) | collective-permute-done | bytes 131104 | tf_op jit(solution)/shard_map/ppermute | solution.py:354
  8.8 3.0 %collective-permute-start.4 = (bf16[256,256]{1,0:T(8,128)(2,1)S(1)}, bf16[256,256]{1,0:T(8,128)(2,1)S(1)}, u32[]{:S(2)}, u32[]{:S(2)}) collective-permute-start(bf16[256,256]{1,0:T(8,128)(2,1)S(1)} %get-tuple-element.22), channel_id=1, source_target_pairs={{0,96},{4,100},{8,104},{12,108},{16,112},{20,116},{24,120},{28,124... | collective-permute-start | bytes 393224 | tf_op jit(solution)/shard_map/ppermute | solution.py:354
  11.8 2.6 %collective-permute-start.2 = (bf16[256,256]{1,0:T(8,128)(2,1)S(1)}, bf16[256,256]{1,0:T(8,128)(2,1)S(1)}, u32[]{:S(2)}, u32[]{:S(2)}) collective-permute-start(bf16[256,256]{1,0:T(8,128)(2,1)S(1)} %get-tuple-element.21), channel_id=1, source_target_pairs={{0,24},{4,28},{8,16},{12,20},{16,8},{20,12},{24,0},{28,4},{32,56},... | collective-permute-start | bytes 393224 | tf_op jit(solution)/shard_map/ppermute | solution.py:354
  14.4 0.0 collective-permute-done.4
  14.4 2.3 %collective-permute-start.5 = (bf16[512,256]{1,0:T(8,128)(2,1)S(1)}, bf16[512,256]{1,0:T(8,128)(2,1)S(1)}, u32[]{:S(2)}, u32[]{:S(2)}) collective-permute-start(bf16[512,256]{1,0:T(8,128)(2,1)S(1)} %pad_maximum_fusion.1), channel_id=1, source_target_pairs={{0,24},{4,28},{8,16},{12,20},{16,8},{20,12},{24,0},{28,4},{32,56},... | collective-permute-start | bytes 786440 | tf_op jit(solution)/shard_map/ppermute | solution.py:354
  16.7 0.5 collective-permute-done.2
  17.2 2.3 %collective-permute-start.3 = (bf16[512,256]{1,0:T(8,128)(2,1)S(1)}, bf16[512,256]{1,0:T(8,128)(2,1)S(1)}, u32[]{:S(2)}, u32[]{:S(2)}) collective-permute-start(bf16[512,256]{1,0:T(8,128)(2,1)S(1)} %pad_maximum_fusion), channel_id=1, source_target_pairs={{0,96},{4,100},{8,104},{12,108},{16,112},{20,116},{24,120},{28,124... | collective-permute-start | bytes 786440 | tf_op jit(solution)/shard_map/ppermute | solution.py:354
  19.6 3.1 %collective-permute-done.5 = bf16[512,256]{1,0:T(8,128)(2,1)S(1)} collective-permute-done((bf16[512,256]{1,0:T(8,128)(2,1)S(1)}, bf16[512,256]{1,0:T(8,128)(2,1)S(1)}, u32[]{:S(2)}, u32[]{:S(2)}) %collective-permute-start.5) | collective-permute-done | bytes 262176 | tf_op jit(solution)/shard_map/ppermute | solution.py:354
  22.7 3.2 %collective-permute-start.9 = (bf16[1024,256]{1,0:T(8,128)(2,1)S(1)}, bf16[1024,256]{1,0:T(8,128)(2,1)S(1)}, u32[]{:S(2)}, u32[]{:S(2)}) collective-permute-start(bf16[1024,256]{1,0:T(8,128)(2,1)S(1)} %constant_dynamic-update-slice_fusion.3.second_ref), channel_id=1, source_target_pairs={{0,4},{4,0},{8,12},{12,8},{16,20},{20,16},{24,28},{28,24},{32,36},... | collective-permute-start | bytes 1572872 | tf_op jit(solution)/shard_map/ppermute | solution.py:354
  25.9 0.0 collective-permute-done.3
  26.0 4.5 %collective-permute-start.8 = (bf16[1024,256]{1,0:T(8,128)(2,1)S(1)}, bf16[1024,256]{1,0:T(8,128)(2,1)S(1)}, u32[]{:S(2)}, u32[]{:S(2)}) collective-permute-start(bf16[1024,256]{1,0:T(8,128)(2,1)S(1)} %constant_dynamic-update-slice_fusion.first_ref), channel_id=1, source_target_pairs={{0,4},{4,0},{8,12},{12,8},{16,20},{20,16},{24,28},{28,24},{32,36},... | collective-permute-start | bytes 1572872 | tf_op jit(solution)/shard_map/ppermute | solution.py:354
  31.2 0.0 collective-permute-done.6
  31.2 3.8 %collective-permute-start.7 = (bf16[256,256]{1,0:T(8,128)(2,1)S(1)}, bf16[256,256]{1,0:T(8,128)(2,1)S(1)}, u32[]{:S(2)}, u32[]{:S(2)}) collective-permute-start(bf16[256,256]{1,0:T(8,128)(2,1)S(1)} %pad_maximum_fusion.7), channel_id=1, source_target_pairs={{0,3},{1,2},{2,1},{3,0},{4,7},{5,6},{6,5},{7,4},{8,11},{9,10},{10,... | collective-permute-start | bytes 393224 | tf_op jit(solution)/shard_map/ppermute | solution.py:354
  35.0 0.0 copy-done.9
  35.0 0.6 shift-right-arithmetic_xor_fusion
  35.6 0.0 copy-start.1
  35.6 0.0 copy-start.7
  35.6 0.0 copy-start.8
  35.6 5.7 %prep.1 = (bf16[65,128,128]{2,1,0:T(8,128)(2,1)}, s32[168]{0:T(256)}, s32[4]{0:T(128)}) custom-call(s32[1]{0:T(128)} %bitcast.22.live_ref, s32[64]{0:T(128)} %get-tuple-element.37.codes, s32[64,128,128]{2,1,0:T(8,128)} %bitcast.25), custom_call_target="tpu_custom_call" | custom-call | flops 1048576 | bytes 6291456 | tf_op jit(solution)/shard_map/prep/pallas_call | solution.py:106
  41.4 0.0 collective-permute-done.7
  41.4 0.0 copy-done.1
  41.4 0.0 copy-done.7
  41.4 0.0 copy-done.8
  41.5 1.0 %project.1 = (bf16[16,128,256]{2,1,0:T(8,128)(2,1)S(1)}, bf16[16,2,144,128]{3,2,1,0:T(8,128)(2,1)S(1)}, bf16[4,2,128,256]{3,2,1,0:T(8,128)(2,1)S(1)}, bf16[256,2...) custom-call(bf16[1024,256]{1,0:T(8,128)(2,1)S(1)} %constant_dynamic-update-slice_fusion.first_ref, ...), custom_call_target="tpu_custom_call" | custom-call | flops 536870912 | bytes 4194304 | tf_op jit(solution)/shard_map/project/pallas_call | solution.py:180
  42.5 0.0 copy-start
  42.5 0.0 copy-start.4
  42.5 0.0 copy-start.5
  42.5 0.0 collective-permute-done.9.second_ref
  42.5 0.0 collective-permute-done.8.first_ref
  42.5 1.1 %join.1 = (bf16[32,128,256]{2,1,0:T(8,128)(2,1)S(1)}, bf16[32,2,144,128]{3,2,1,0:T(8,128)(2,1)S(1)}) custom-call(bf16[1024,256]{1,0:T(8,128)(2,1)S(1)} %collective-permute-done.8.first_ref, bf16[1024,256]{1,0:T(8,128)(2,1)S(1)} %collective-permute-done.9.second_ref, bf16[256,256]{1,0:T(8,128)(2,1)S(1)} %copy-done.1, ...), custom_call_target="tpu_custom_call" | custom-call | flops 536870912 | bytes 4194304 | tf_op jit(solution)/shard_map/join/pallas_call | solution.py:271
  43.6 0.5 copy-done
  44.1 0.0 copy-done.4
  44.1 0.0 copy-done.5
  44.1 2.8 %shard_map.93 = bf16[288,128]{1,0:T(8,128)(2,1)S(1)} custom-call(s32[72]{0:T(128)S(1)} %concatenate.37.spot_list, s32[168]{0:T(256)S(1)} %copy-done.4, s32[4]{0:T(128)S(1)} %copy-done.5, bf16[65,128,128]{2,1,0:T(8,128)(2,1)S(1)} %copy-done, bf16[4,2,128,256]{3,2,1,0:T(8,128)(2,1)S(1)} %get-tuple-element.23.query_ref, ...), custom_call_target="tpu_custom_call" | custom-call | flops 1073741824 | bytes 8388608 | tf_op jit(solution)/shard_map/pallas_call | solution.py:289
  46.9 2.6 %shard_map.92 = bf16[288,128]{1,0:T(8,128)(2,1)S(1)} custom-call(s32[72]{0:T(128)S(1)} %concatenate.37.spot_list, s32[168]{0:T(256)S(1)} %copy-done.4, s32[4]{0:T(128)S(1)} %copy-done.5, bf16[65,128,128]{2,1,0:T(8,128)(2,1)S(1)} %copy-done, bf16[4,2,128,256]{3,2,1,0:T(8,128)(2,1)S(1)} %get-tuple-element.23.query_ref, ...), custom_call_target="tpu_custom_call" | custom-call | flops 1073741824 | bytes 8388608 | tf_op jit(solution)/shard_map/pallas_call | solution.py:289
  49.5 3.0 %shard_map.91 = bf16[288,128]{1,0:T(8,128)(2,1)S(1)} custom-call(s32[72]{0:T(128)S(1)} %concatenate.37.spot_list, s32[168]{0:T(256)S(1)} %copy-done.4, s32[4]{0:T(128)S(1)} %copy-done.5, bf16[65,128,128]{2,1,0:T(8,128)(2,1)S(1)} %copy-done, bf16[4,2,128,256]{3,2,1,0:T(8,128)(2,1)S(1)} %get-tuple-element.23.query_ref, ...), custom_call_target="tpu_custom_call" | custom-call | flops 1073741824 | bytes 8388608 | tf_op jit(solution)/shard_map/pallas_call | solution.py:289
  52.5 0.0 copy-start.2
  52.5 0.0 copy-start.6
  52.5 0.1 collective-permute-start.12
  52.6 0.1 collective-permute-start.11
  52.7 3.1 %collective-permute-start.10 = (bf16[288,128]{1,0:T(8,128)(2,1)S(1)}, bf16[288,128]{1,0:T(8,128)(2,1)S(1)}, u32[]{:S(2)}, u32[]{:S(2)}) collective-permute-start(bf16[288,128]{1,0:T(8,128)(2,1)S(1)} %shard_map.91), channel_id=1, source_target_pairs={{0,2},{1,3},{2,0},{3,1},{4,6},{5,7},{6,4},{7,5},{8,10},{9,11},{10,... | collective-permute-start | bytes 221192 | tf_op jit(solution)/shard_map/ppermute | solution.py:354
  55.9 3.0 %shard_map.94.part3 = bf16[288,128]{1,0:T(8,128)(2,1)S(1)} custom-call(s32[72]{0:T(128)S(1)} %concatenate.37.spot_list, s32[168]{0:T(256)S(1)} %copy-done.4, s32[4]{0:T(128)S(1)} %copy-done.5, bf16[65,128,128]{2,1,0:T(8,128)(2,1)S(1)} %copy-done, bf16[4,2,128,256]{3,2,1,0:T(8,128)(2,1)S(1)} %get-tuple-element.23.query_ref, ...), custom_call_target="tpu_custom_call" | custom-call | flops 1073741824 | bytes 8388608 | tf_op jit(solution)/shard_map/pallas_call | solution.py:289
  58.8 0.0 collective-permute-done.12.part2
  58.8 0.6 collective-permute-done.11.part1
  59.4 0.0 collective-permute-done.10.part0
  59.4 0.0 copy-done.2
  59.4 0.0 copy-done.6
  59.4 1.2 %finish.1 = bf16[128,256]{1,0:T(8,128)(2,1)} custom-call(bf16[288,128]{1,0:T(8,128)(2,1)S(1)} %collective-permute-done.10.part0, bf16[288,128]{1,0:T(8,128)(2,1)S(1)} %collective-permute-done.11.part1, bf16[288,128]{1,0:T(8,128)(2,1)S(1)} %collective-permute-done.12.part2, bf16[288,128]{1,0:T(8,128)(2,1)S(1)} %shard_map.94.part3, ...), custom_call_target="tpu_custom_call" | custom-call | flops 67108864 | bytes 1048576 | tf_op jit(solution)/shard_map/finish/pallas_call | solution.py:342
  (16 shorter events, 0.2 us)
Async XLA Ops:
  0.0 0.8 %copy-start.3 = (bf16[128,256]{1,0:T(8,128)(2,1)S(1)}, bf16[128,256]{1,0:T(8,128)(2,1)}, u32[]{:S(2)}) copy-start(bf16[128,256]{1,0:T(8,128)(2,1)} %points_ref.1) | copy-start | bytes 196612
  1.0 3.8 %collective-permute-start = (bf16[128,256]{1,0:T(8,128)(2,1)S(1)}, bf16[128,256]{1,0:T(8,128)(2,1)S(1)}, u32[]{:S(2)}, u32[]{:S(2)}) collective-permute-start(bf16[128,256]{1,0:T(8,128)(2,1)S(1)} %tangent.1.tangent_ref), channel_id=1, source_target_pairs={{0,8},{4,12},{8,0},{12,4},{16,24},{20,28},{24,16},{28,20},{32,40},... | collective-permute-start | bytes 196616 | tf_op jit(solution)/shard_map/ppermute | solution.py:354
  4.8 30.2 %copy-start.9 = (s32[1,1,64]{2,1,0:T(1,128)S(1)}, s32[1,1,64]{2,1,0:T(1,128)}, u32[]{:S(2)}) copy-start(s32[1,1,64]{2,1,0:T(1,128)} %param.16) | copy-start | bytes 772
  4.8 4.0 %collective-permute-start.1 = (bf16[256,256]{1,0:T(8,128)(2,1)S(1)}, bf16[256,256]{1,0:T(8,128)(2,1)S(1)}, u32[]{:S(2)}, u32[]{:S(2)}) collective-permute-start(bf16[256,256]{1,0:T(8,128)(2,1)S(1)} %pad_maximum_fusion.3), channel_id=1, source_target_pairs={{0,32},{4,36},{8,40},{12,44},{16,48},{20,52},{24,56},{28,60},{32,0... | collective-permute-start | bytes 393224 | tf_op jit(solution)/shard_map/ppermute | solution.py:354
  6.4 24.7 %collective-permute-start.6 = (bf16[128,256]{1,0:T(8,128)(2,1)S(1)}, bf16[128,256]{1,0:T(8,128)(2,1)S(1)}, u32[]{:S(2)}, u32[]{:S(2)}) collective-permute-start(bf16[128,256]{1,0:T(8,128)(2,1)S(1)} %tangent.1.tangent_ref), channel_id=1, source_target_pairs={{0,1},{1,0},{2,3},{3,2},{4,5},{5,4},{6,7},{7,6},{8,9},{9,8},{10,11... | collective-permute-start | bytes 196616 | tf_op jit(solution)/shard_map/ppermute | solution.py:354
  8.8 5.6 %collective-permute-start.4 = (bf16[256,256]{1,0:T(8,128)(2,1)S(1)}, bf16[256,256]{1,0:T(8,128)(2,1)S(1)}, u32[]{:S(2)}, u32[]{:S(2)}) collective-permute-start(bf16[256,256]{1,0:T(8,128)(2,1)S(1)} %get-tuple-element.22), channel_id=1, source_target_pairs={{0,96},{4,100},{8,104},{12,108},{16,112},{20,116},{24,120},{28,124... | collective-permute-start | bytes 393224 | tf_op jit(solution)/shard_map/ppermute | solution.py:354
  11.8 5.4 %collective-permute-start.2 = (bf16[256,256]{1,0:T(8,128)(2,1)S(1)}, bf16[256,256]{1,0:T(8,128)(2,1)S(1)}, u32[]{:S(2)}, u32[]{:S(2)}) collective-permute-start(bf16[256,256]{1,0:T(8,128)(2,1)S(1)} %get-tuple-element.21), channel_id=1, source_target_pairs={{0,24},{4,28},{8,16},{12,20},{16,8},{20,12},{24,0},{28,4},{32,56},... | collective-permute-start | bytes 393224 | tf_op jit(solution)/shard_map/ppermute | solution.py:354
  14.4 8.3 %collective-permute-start.5 = (bf16[512,256]{1,0:T(8,128)(2,1)S(1)}, bf16[512,256]{1,0:T(8,128)(2,1)S(1)}, u32[]{:S(2)}, u32[]{:S(2)}) collective-permute-start(bf16[512,256]{1,0:T(8,128)(2,1)S(1)} %pad_maximum_fusion.1), channel_id=1, source_target_pairs={{0,24},{4,28},{8,16},{12,20},{16,8},{20,12},{24,0},{28,4},{32,56},... | collective-permute-start | bytes 786440 | tf_op jit(solution)/shard_map/ppermute | solution.py:354
  17.2 8.7 %collective-permute-start.3 = (bf16[512,256]{1,0:T(8,128)(2,1)S(1)}, bf16[512,256]{1,0:T(8,128)(2,1)S(1)}, u32[]{:S(2)}, u32[]{:S(2)}) collective-permute-start(bf16[512,256]{1,0:T(8,128)(2,1)S(1)} %pad_maximum_fusion), channel_id=1, source_target_pairs={{0,96},{4,100},{8,104},{12,108},{16,112},{20,116},{24,120},{28,124... | collective-permute-start | bytes 786440 | tf_op jit(solution)/shard_map/ppermute | solution.py:354
  22.7 19.8 %collective-permute-start.9 = (bf16[1024,256]{1,0:T(8,128)(2,1)S(1)}, bf16[1024,256]{1,0:T(8,128)(2,1)S(1)}, u32[]{:S(2)}, u32[]{:S(2)}) collective-permute-start(bf16[1024,256]{1,0:T(8,128)(2,1)S(1)} %constant_dynamic-update-slice_fusion.3.second_ref), channel_id=1, source_target_pairs={{0,4},{4,0},{8,12},{12,8},{16,20},{20,16},{24,28},{28,24},{32,36},... | collective-permute-start | bytes 1572872 | tf_op jit(solution)/shard_map/ppermute | solution.py:354
  26.0 16.5 %collective-permute-start.8 = (bf16[1024,256]{1,0:T(8,128)(2,1)S(1)}, bf16[1024,256]{1,0:T(8,128)(2,1)S(1)}, u32[]{:S(2)}, u32[]{:S(2)}) collective-permute-start(bf16[1024,256]{1,0:T(8,128)(2,1)S(1)} %constant_dynamic-update-slice_fusion.first_ref), channel_id=1, source_target_pairs={{0,4},{4,0},{8,12},{12,8},{16,20},{20,16},{24,28},{28,24},{32,36},... | collective-permute-start | bytes 1572872 | tf_op jit(solution)/shard_map/ppermute | solution.py:354
  31.2 10.2 %collective-permute-start.7 = (bf16[256,256]{1,0:T(8,128)(2,1)S(1)}, bf16[256,256]{1,0:T(8,128)(2,1)S(1)}, u32[]{:S(2)}, u32[]{:S(2)}) collective-permute-start(bf16[256,256]{1,0:T(8,128)(2,1)S(1)} %pad_maximum_fusion.7), channel_id=1, source_target_pairs={{0,3},{1,2},{2,1},{3,0},{4,7},{5,6},{6,5},{7,4},{8,11},{9,10},{10,... | collective-permute-start | bytes 393224 | tf_op jit(solution)/shard_map/ppermute | solution.py:354
  35.6 5.8 %copy-start.1 = (bf16[256,256]{1,0:T(8,128)(2,1)S(1)}, bf16[256,256]{1,0:T(8,128)(2,1)}, u32[]{:S(2)}) copy-start(bf16[256,256]{1,0:T(8,128)(2,1)} %wk_ref.3) | copy-start | bytes 393220
  35.6 5.8 %copy-start.7 = (bf16[256,256]{1,0:T(8,128)(2,1)S(1)}, bf16[256,256]{1,0:T(8,128)(2,1)}, u32[]{:S(2)}) copy-start(bf16[256,256]{1,0:T(8,128)(2,1)} %wq_ref.1) | copy-start | bytes 393220
  35.6 5.8 %copy-start.8 = (bf16[256,256]{1,0:T(8,128)(2,1)S(1)}, bf16[256,256]{1,0:T(8,128)(2,1)}, u32[]{:S(2)}) copy-start(bf16[256,256]{1,0:T(8,128)(2,1)} %wv_ref.1) | copy-start | bytes 393220
  42.5 1.6 %copy-start = (bf16[65,128,128]{2,1,0:T(8,128)(2,1)S(1)}, bf16[65,128,128]{2,1,0:T(8,128)(2,1)}, u32[]{:S(2)}) copy-start(bf16[65,128,128]{2,1,0:T(8,128)(2,1)} %get-tuple-element.20.bias_ref) | copy-start | bytes 6389764
  42.5 1.6 %copy-start.4 = (s32[168]{0:T(256)S(1)}, s32[168]{0:T(256)}, u32[]{:S(2)}) copy-start(s32[168]{0:T(256)} %get-tuple-element.18.tile_list) | copy-start | bytes 2020
  42.5 1.6 %copy-start.5 = (s32[4]{0:T(128)S(1)}, s32[4]{0:T(128)}, u32[]{:S(2)}) copy-start(s32[4]{0:T(128)} %get-tuple-element.19.counts) | copy-start | bytes 52
  52.5 6.9 %copy-start.2 = (bf16[256,256]{1,0:T(8,128)(2,1)S(1)}, bf16[256,256]{1,0:T(8,128)(2,1)}, u32[]{:S(2)}) copy-start(bf16[256,256]{1,0:T(8,128)(2,1)} %wo_ref.1) | copy-start | bytes 393220
  52.5 6.9 %copy-start.6 = (f32[256]{0:T(256)S(1)}, f32[256]{0:T(256)}, u32[]{:S(2)}) copy-start(f32[256]{0:T(256)} %param.14) | copy-start | bytes 3076
  52.5 6.3 %collective-permute-start.12 = (bf16[288,128]{1,0:T(8,128)(2,1)S(1)}, bf16[288,128]{1,0:T(8,128)(2,1)S(1)}, u32[]{:S(2)}, u32[]{:S(2)}) collective-permute-start(bf16[288,128]{1,0:T(8,128)(2,1)S(1)} %shard_map.93), channel_id=1, source_target_pairs={{0,1},{1,0},{2,3},{3,2},{4,5},{5,4},{6,7},{7,6},{8,9},{9,8},{10,11... | collective-permute-start | bytes 221192 | tf_op jit(solution)/shard_map/ppermute | solution.py:354
  52.6 6.8 %collective-permute-start.11 = (bf16[288,128]{1,0:T(8,128)(2,1)S(1)}, bf16[288,128]{1,0:T(8,128)(2,1)S(1)}, u32[]{:S(2)}, u32[]{:S(2)}) collective-permute-start(bf16[288,128]{1,0:T(8,128)(2,1)S(1)} %shard_map.92), channel_id=1, source_target_pairs={{0,3},{1,2},{2,1},{3,0},{4,7},{5,6},{6,5},{7,4},{8,11},{9,10},{10,... | collective-permute-start | bytes 221192 | tf_op jit(solution)/shard_map/ppermute | solution.py:354
  52.7 6.7 %collective-permute-start.10 = (bf16[288,128]{1,0:T(8,128)(2,1)S(1)}, bf16[288,128]{1,0:T(8,128)(2,1)S(1)}, u32[]{:S(2)}, u32[]{:S(2)}) collective-permute-start(bf16[288,128]{1,0:T(8,128)(2,1)S(1)} %shard_map.91), channel_id=1, source_target_pairs={{0,2},{1,3},{2,0},{3,1},{4,6},{5,7},{6,4},{7,5},{8,10},{9,11},{10,... | collective-permute-start | bytes 221192 | tf_op jit(solution)/shard_map/ppermute | solution.py:354
where the time goes:
time: 60.8 us; the launch traced here: 60.6 us
  starting transfers between devices  30.4 us (50%)
  Pallas kernels  20.5 us (34%)
  waiting for transfers between devices  6.61 us (11%)
  local copies, waits for them, and re-layouts  1.46 us (2%)
  between operations  0.92 us (2%)
  other arithmetic  0.68 us (1%)
    ppermute x13, starting transfers between devices, swap(): return lax.ppermute(value, axis, [(at, at ^ mask) for at in range(size)])  30.4 us
    pallas_call x4, Pallas kernels, attend(): pl.pallas_call(functools.partial(attend_rows, group), in_specs=[sm] * 3 +...  11.4 us
    ppermute x13, waiting for transfers between devices, swap(): return lax.ppermute(value, axis, [(at, at ^ mask) for at in range(size)])  6.61 us
    pallas_call x1, Pallas kernels, prepare(): pl.pallas_call(prep_kernel, in_specs=[sm, sm, pl.BlockSpec(memory_space=p...  5.74 us
    unnamed x24, local copies, waits for them, and re-layouts  1.4 us
  transfers between devices with their start and end apart: 13, of which 5 were waited for; matrix products, arithmetic and copies ran while one was open for 1% of the time, Pallas kernels for 16%

commit v1 on v0

--- a/solution.py
+++ b/solution.py
@@ -16,7 +16,6 @@
 FLOOR = -1e29
 PREP = 8
 QUAD = 4
-OCT = 8
 STRIDE = 40
 F32 = jnp.float32
 BF16 = jnp.bfloat16
@@ -200,11 +199,13 @@
 ):
     base = group * STRIDE
     count = counts[group]
-    most = count // OCT
-    quads = (count - most * OCT + 1) // QUAD
-    quad_at = most * OCT
-    rest_at = quad_at + quads * QUAD
-    rest = (count - rest_at + 1) // 2
+    ladder = []
+    done = jnp.int32(0)
+    for size in (16, 8, 4, 2):
+        pad = 1 if size <= QUAD else 0
+        trips = (count - done + pad) // size
+        ladder.append((size, done, trips))
+        done = done + trips * size
 
     def score(start, size, tops):
         tops = list(tops)
@@ -221,9 +222,9 @@
         return tuple(tops)
 
     floor = jnp.full((8, PAIR), FLOOR, F32)
-    tops = lax.fori_loop(0, most, lambda trip, tops: score(trip * OCT, OCT, tops), (floor, floor))
-    tops = lax.fori_loop(0, quads, lambda trip, tops: score(quad_at + trip * QUAD, QUAD, tops), tops)
-    tops = lax.fori_loop(0, rest, lambda trip, tops: score(rest_at + trip * 2, 2, tops), tops)
+    tops = (floor, floor)
+    for size, start, trips in ladder:
+        tops = lax.fori_loop(0, trips, lambda trip, tops: score(start + trip * size, size, tops), tops)
     tops = [jnp.max(top, axis=0, keepdims=True) for top in tops]
     acc_ref[...] = jnp.zeros(acc_ref.shape, F32)
 
@@ -235,9 +236,8 @@
             acc_ref[half] += jnp.dot(values, jnp.concatenate(weights, axis=0), preferred_element_type=F32)
         return 0
 
-    lax.fori_loop(0, most, lambda trip, _: mix(trip * OCT, OCT), 0)
-    lax.fori_loop(0, quads, lambda trip, _: mix(quad_at + trip * QUAD, QUAD), 0)
-    lax.fori_loop(0, rest, lambda trip, _: mix(rest_at + trip * 2, 2), 0)
+    for size, start, trips in ladder:
+        lax.fori_loop(0, trips, lambda trip, _: mix(start + trip * size, size), 0)
     for half in range(2):
         acc = acc_ref[half]
         part_ref[pl.ds(half * TILE, 64), :] = acc[:64, :TILE].astype(BF16)

time: 60.8 us -> 61.1 us (level)
  no operation moved by 1% of the time
where the time goes in v1:
time: 61.1 us; the launch traced here: 60.9 us
  starting transfers between devices  30.4 us (50%)
  Pallas kernels  20.2 us (33%)
  waiting for transfers between devices  7.19 us (12%)
  local copies, waits for them, and re-layouts  1.46 us (2%)
  between operations  0.92 us (2%)
  other arithmetic  0.68 us (1%)
    ppermute x13, starting transfers between devices, swap(): return lax.ppermute(value, axis, [(at, at ^ mask) for at in range(size)])  30.4 us
    pallas_call x4, Pallas kernels, attend(): pl.pallas_call(functools.partial(attend_rows, group), in_specs=[sm] * 3 +...  11 us
    ppermute x13, waiting for transfers between devices, swap(): return lax.ppermute(value, axis, [(at, at ^ mask) for at in range(size)])  7.19 us
    pallas_call x1, Pallas kernels, prepare(): pl.pallas_call(prep_kernel, in_specs=[sm, sm, pl.BlockSpec(memory_space=p...  5.74 us
    unnamed x24, local copies, waits for them, and re-layouts  1.41 us
  transfers between devices with their start and end apart: 13, of which 5 were waited for; matrix products, arithmetic and copies ran while one was open for 1% of the time, Pallas kernels for 16%

profile of v1, /device:TPU:1, one launch (start us, length us, event | category | flops | bytes accessed | tf_op | source)
XLA Modules:
  0.0 60.9 jit_solution(1980178474028861247)
XLA Ops:
  0.0 0.0 copy-start.3
  0.0 0.8 %copy-done.3 = bf16[128,256]{1,0:T(8,128)(2,1)S(1)} copy-done((bf16[128,256]{1,0:T(8,128)(2,1)S(1)}, bf16[128,256]{1,0:T(8,128)(2,1)}, u32[]{:S(2)}) %copy-start.3) | copy-done | bytes 65560
  0.8 0.2 tangent.1.tangent_ref
  1.0 2.1 %collective-permute-start = (bf16[128,256]{1,0:T(8,128)(2,1)S(1)}, bf16[128,256]{1,0:T(8,128)(2,1)S(1)}, u32[]{:S(2)}, u32[]{:S(2)}) collective-permute-start(bf16[128,256]{1,0:T(8,128)(2,1)S(1)} %tangent.1.tangent_ref), channel_id=1, source_target_pairs={{0,8},{4,12},{8,0},{12,4},{16,24},{20,28},{24,16},{28,20},{32,40},... | collective-permute-start | bytes 196616 | tf_op jit(solution)/shard_map/ppermute | solution.py:354
  3.1 1.6 %collective-permute-done = bf16[128,256]{1,0:T(8,128)(2,1)S(1)} collective-permute-done((bf16[128,256]{1,0:T(8,128)(2,1)S(1)}, bf16[128,256]{1,0:T(8,128)(2,1)S(1)}, u32[]{:S(2)}, u32[]{:S(2)}) %collective-permute-start) | collective-permute-done | bytes 65568 | tf_op jit(solution)/shard_map/ppermute | solution.py:354
  4.8 0.0 copy-start.9
  4.8 1.6 %collective-permute-start.1 = (bf16[256,256]{1,0:T(8,128)(2,1)S(1)}, bf16[256,256]{1,0:T(8,128)(2,1)S(1)}, u32[]{:S(2)}, u32[]{:S(2)}) collective-permute-start(bf16[256,256]{1,0:T(8,128)(2,1)S(1)} %pad_maximum_fusion.3), channel_id=1, source_target_pairs={{0,32},{4,36},{8,40},{12,44},{16,48},{20,52},{24,56},{28,60},{32,0... | collective-permute-start | bytes 393224 | tf_op jit(solution)/shard_map/ppermute | solution.py:354
  6.4 1.6 %collective-permute-start.6 = (bf16[128,256]{1,0:T(8,128)(2,1)S(1)}, bf16[128,256]{1,0:T(8,128)(2,1)S(1)}, u32[]{:S(2)}, u32[]{:S(2)}) collective-permute-start(bf16[128,256]{1,0:T(8,128)(2,1)S(1)} %tangent.1.tangent_ref), channel_id=1, source_target_pairs={{0,1},{1,0},{2,3},{3,2},{4,5},{5,4},{6,7},{7,6},{8,9},{9,8},{10,11... | collective-permute-start | bytes 196616 | tf_op jit(solution)/shard_map/ppermute | solution.py:354
  8.1 0.7 %collective-permute-done.1 = bf16[256,256]{1,0:T(8,128)(2,1)S(1)} collective-permute-done((bf16[256,256]{1,0:T(8,128)(2,1)S(1)}, bf16[256,256]{1,0:T(8,128)(2,1)S(1)}, u32[]{:S(2)}, u32[]{:S(2)}) %collective-permute-start.1) | collective-permute-done | bytes 131104 | tf_op jit(solution)/shard_map/ppermute | solution.py:354
  8.8 3.0 %collective-permute-start.4 = (bf16[256,256]{1,0:T(8,128)(2,1)S(1)}, bf16[256,256]{1,0:T(8,128)(2,1)S(1)}, u32[]{:S(2)}, u32[]{:S(2)}) collective-permute-start(bf16[256,256]{1,0:T(8,128)(2,1)S(1)} %get-tuple-element.22), channel_id=1, source_target_pairs={{0,96},{4,100},{8,104},{12,108},{16,112},{20,116},{24,120},{28,124... | collective-permute-start | bytes 393224 | tf_op jit(solution)/shard_map/ppermute | solution.py:354
  11.8 2.6 %collective-permute-start.2 = (bf16[256,256]{1,0:T(8,128)(2,1)S(1)}, bf16[256,256]{1,0:T(8,128)(2,1)S(1)}, u32[]{:S(2)}, u32[]{:S(2)}) collective-permute-start(bf16[256,256]{1,0:T(8,128)(2,1)S(1)} %get-tuple-element.21), channel_id=1, source_target_pairs={{0,24},{4,28},{8,16},{12,20},{16,8},{20,12},{24,0},{28,4},{32,56},... | collective-permute-start | bytes 393224 | tf_op jit(solution)/shard_map/ppermute | solution.py:354
  14.4 0.0 collective-permute-done.4
  14.4 2.3 %collective-permute-start.5 = (bf16[512,256]{1,0:T(8,128)(2,1)S(1)}, bf16[512,256]{1,0:T(8,128)(2,1)S(1)}, u32[]{:S(2)}, u32[]{:S(2)}) collective-permute-start(bf16[512,256]{1,0:T(8,128)(2,1)S(1)} %pad_maximum_fusion.1), channel_id=1, source_target_pairs={{0,24},{4,28},{8,16},{12,20},{16,8},{20,12},{24,0},{28,4},{32,56},... | collective-permute-start | bytes 786440 | tf_op jit(solution)/shard_map/ppermute | solution.py:354
  16.7 0.5 collective-permute-done.2
  17.2 2.3 %collective-permute-start.3 = (bf16[512,256]{1,0:T(8,128)(2,1)S(1)}, bf16[512,256]{1,0:T(8,128)(2,1)S(1)}, u32[]{:S(2)}, u32[]{:S(2)}) collective-permute-start(bf16[512,256]{1,0:T(8,128)(2,1)S(1)} %pad_maximum_fusion), channel_id=1, source_target_pairs={{0,96},{4,100},{8,104},{12,108},{16,112},{20,116},{24,120},{28,124... | collective-permute-start | bytes 786440 | tf_op jit(solution)/shard_map/ppermute | solution.py:354
  19.6 3.1 %collective-permute-done.5 = bf16[512,256]{1,0:T(8,128)(2,1)S(1)} collective-permute-done((bf16[512,256]{1,0:T(8,128)(2,1)S(1)}, bf16[512,256]{1,0:T(8,128)(2,1)S(1)}, u32[]{:S(2)}, u32[]{:S(2)}) %collective-permute-start.5) | collective-permute-done | bytes 262176 | tf_op jit(solution)/shard_map/ppermute | solution.py:354
  22.7 3.2 %collective-permute-start.9 = (bf16[1024,256]{1,0:T(8,128)(2,1)S(1)}, bf16[1024,256]{1,0:T(8,128)(2,1)S(1)}, u32[]{:S(2)}, u32[]{:S(2)}) collective-permute-start(bf16[1024,256]{1,0:T(8,128)(2,1)S(1)} %constant_dynamic-update-slice_fusion.3.second_ref), channel_id=1, source_target_pairs={{0,4},{4,0},{8,12},{12,8},{16,20},{20,16},{24,28},{28,24},{32,36},... | collective-permute-start | bytes 1572872 | tf_op jit(solution)/shard_map/ppermute | solution.py:354
  25.9 0.0 collective-permute-done.3
  26.0 4.5 %collective-permute-start.8 = (bf16[1024,256]{1,0:T(8,128)(2,1)S(1)}, bf16[1024,256]{1,0:T(8,128)(2,1)S(1)}, u32[]{:S(2)}, u32[]{:S(2)}) collective-permute-start(bf16[1024,256]{1,0:T(8,128)(2,1)S(1)} %constant_dynamic-update-slice_fusion.first_ref), channel_id=1, source_target_pairs={{0,4},{4,0},{8,12},{12,8},{16,20},{20,16},{24,28},{28,24},{32,36},... | collective-permute-start | bytes 1572872 | tf_op jit(solution)/shard_map/ppermute | solution.py:354
  31.2 0.0 collective-permute-done.6
  31.2 3.8 %collective-permute-start.7 = (bf16[256,256]{1,0:T(8,128)(2,1)S(1)}, bf16[256,256]{1,0:T(8,128)(2,1)S(1)}, u32[]{:S(2)}, u32[]{:S(2)}) collective-permute-start(bf16[256,256]{1,0:T(8,128)(2,1)S(1)} %pad_maximum_fusion.7), channel_id=1, source_target_pairs={{0,3},{1,2},{2,1},{3,0},{4,7},{5,6},{6,5},{7,4},{8,11},{9,10},{10,... | collective-permute-start | bytes 393224 | tf_op jit(solution)/shard_map/ppermute | solution.py:354
  35.0 0.0 copy-done.9
  35.0 0.6 shift-right-arithmetic_xor_fusion
  35.6 0.0 copy-start.1
  35.6 0.0 copy-start.7
  35.6 0.0 copy-start.8
  35.6 5.7 %prep.1 = (bf16[65,128,128]{2,1,0:T(8,128)(2,1)}, s32[168]{0:T(256)}, s32[4]{0:T(128)}) custom-call(s32[1]{0:T(128)} %bitcast.22.live_ref, s32[64]{0:T(128)} %get-tuple-element.37.codes, s32[64,128,128]{2,1,0:T(8,128)} %bitcast.25), custom_call_target="tpu_custom_call" | custom-call | flops 1048576 | bytes 6291456 | tf_op jit(solution)/shard_map/prep/pallas_call | solution.py:105
  41.4 0.0 collective-permute-done.7
  41.4 0.0 copy-done.1
  41.4 0.0 copy-done.7
  41.4 0.0 copy-done.8
  41.5 1.0 %project.1 = (bf16[16,128,256]{2,1,0:T(8,128)(2,1)S(1)}, bf16[16,2,144,128]{3,2,1,0:T(8,128)(2,1)S(1)}, bf16[4,2,128,256]{3,2,1,0:T(8,128)(2,1)S(1)}, bf16[256,2...) custom-call(bf16[1024,256]{1,0:T(8,128)(2,1)S(1)} %constant_dynamic-update-slice_fusion.first_ref, ...), custom_call_target="tpu_custom_call" | custom-call | flops 536870912 | bytes 4194304 | tf_op jit(solution)/shard_map/project/pallas_call | solution.py:179
  42.5 0.0 copy-start
  42.5 0.0 copy-start.4
  42.5 0.0 copy-start.5
  42.5 0.0 collective-permute-done.9.second_ref
  42.5 0.0 collective-permute-done.8.first_ref
  42.5 1.1 %join.1 = (bf16[32,128,256]{2,1,0:T(8,128)(2,1)S(1)}, bf16[32,2,144,128]{3,2,1,0:T(8,128)(2,1)S(1)}) custom-call(bf16[1024,256]{1,0:T(8,128)(2,1)S(1)} %collective-permute-done.8.first_ref, bf16[1024,256]{1,0:T(8,128)(2,1)S(1)} %collective-permute-done.9.second_ref, bf16[256,256]{1,0:T(8,128)(2,1)S(1)} %copy-done.1, ...), custom_call_target="tpu_custom_call" | custom-call | flops 536870912 | bytes 4194304 | tf_op jit(solution)/shard_map/join/pallas_call | solution.py:271
  43.6 0.5 copy-done
  44.1 0.0 copy-done.4
  44.1 0.0 copy-done.5
  44.1 2.8 %shard_map.93 = bf16[288,128]{1,0:T(8,128)(2,1)S(1)} custom-call(s32[72]{0:T(128)S(1)} %concatenate.37.spot_list, s32[168]{0:T(256)S(1)} %copy-done.4, s32[4]{0:T(128)S(1)} %copy-done.5, bf16[65,128,128]{2,1,0:T(8,128)(2,1)S(1)} %copy-done, bf16[4,2,128,256]{3,2,1,0:T(8,128)(2,1)S(1)} %get-tuple-element.23.query_ref, ...), custom_call_target="tpu_custom_call" | custom-call | flops 1073741824 | bytes 8388608 | tf_op jit(solution)/shard_map/pallas_call | solution.py:289
  46.9 2.7 %shard_map.92 = bf16[288,128]{1,0:T(8,128)(2,1)S(1)} custom-call(s32[72]{0:T(128)S(1)} %concatenate.37.spot_list, s32[168]{0:T(256)S(1)} %copy-done.4, s32[4]{0:T(128)S(1)} %copy-done.5, bf16[65,128,128]{2,1,0:T(8,128)(2,1)S(1)} %copy-done, bf16[4,2,128,256]{3,2,1,0:T(8,128)(2,1)S(1)} %get-tuple-element.23.query_ref, ...), custom_call_target="tpu_custom_call" | custom-call | flops 1073741824 | bytes 8388608 | tf_op jit(solution)/shard_map/pallas_call | solution.py:289
  49.6 2.9 %shard_map.91 = bf16[288,128]{1,0:T(8,128)(2,1)S(1)} custom-call(s32[72]{0:T(128)S(1)} %concatenate.37.spot_list, s32[168]{0:T(256)S(1)} %copy-done.4, s32[4]{0:T(128)S(1)} %copy-done.5, bf16[65,128,128]{2,1,0:T(8,128)(2,1)S(1)} %copy-done, bf16[4,2,128,256]{3,2,1,0:T(8,128)(2,1)S(1)} %get-tuple-element.23.query_ref, ...), custom_call_target="tpu_custom_call" | custom-call | flops 1073741824 | bytes 8388608 | tf_op jit(solution)/shard_map/pallas_call | solution.py:289
  52.4 0.0 copy-start.2
  52.5 0.0 copy-start.6
  52.5 0.1 collective-permute-start.12
  52.6 0.1 collective-permute-start.11
  52.7 3.1 %collective-permute-start.10 = (bf16[288,128]{1,0:T(8,128)(2,1)S(1)}, bf16[288,128]{1,0:T(8,128)(2,1)S(1)}, u32[]{:S(2)}, u32[]{:S(2)}) collective-permute-start(bf16[288,128]{1,0:T(8,128)(2,1)S(1)} %shard_map.91), channel_id=1, source_target_pairs={{0,2},{1,3},{2,0},{3,1},{4,6},{5,7},{6,4},{7,5},{8,10},{9,11},{10,... | collective-permute-start | bytes 221192 | tf_op jit(solution)/shard_map/ppermute | solution.py:354
  55.8 2.7 %shard_map.94.part3 = bf16[288,128]{1,0:T(8,128)(2,1)S(1)} custom-call(s32[72]{0:T(128)S(1)} %concatenate.37.spot_list, s32[168]{0:T(256)S(1)} %copy-done.4, s32[4]{0:T(128)S(1)} %copy-done.5, bf16[65,128,128]{2,1,0:T(8,128)(2,1)S(1)} %copy-done, bf16[4,2,128,256]{3,2,1,0:T(8,128)(2,1)S(1)} %get-tuple-element.23.query_ref, ...), custom_call_target="tpu_custom_call" | custom-call | flops 1073741824 | bytes 8388608 | tf_op jit(solution)/shard_map/pallas_call | solution.py:289
  58.5 0.0 collective-permute-done.12.part2
  58.5 1.2 %collective-permute-done.11.part1 = bf16[288,128]{1,0:T(8,128)(2,1)S(1)} collective-permute-done((bf16[288,128]{1,0:T(8,128)(2,1)S(1)}, bf16[288,128]{1,0:T(8,128)(2,1)S(1)}, u32[]{:S(2)}, u32[]{:S(2)}) %collective-permute-start.11) | collective-permute-done | bytes 73760 | tf_op jit(solution)/shard_map/ppermute | solution.py:354
  59.7 0.0 collective-permute-done.10.part0
  59.7 0.0 copy-done.2
  59.7 0.0 copy-done.6
  59.7 1.2 %finish.1 = bf16[128,256]{1,0:T(8,128)(2,1)} custom-call(bf16[288,128]{1,0:T(8,128)(2,1)S(1)} %collective-permute-done.10.part0, bf16[288,128]{1,0:T(8,128)(2,1)S(1)} %collective-permute-done.11.part1, bf16[288,128]{1,0:T(8,128)(2,1)S(1)} %collective-permute-done.12.part2, bf16[288,128]{1,0:T(8,128)(2,1)S(1)} %shard_map.94.part3, ...), custom_call_target="tpu_custom_call" | custom-call | flops 67108864 | bytes 1048576 | tf_op jit(solution)/shard_map/finish/pallas_call | solution.py:342
  (16 shorter events, 0.2 us)
Async XLA Ops:
  0.0 0.8 %copy-start.3 = (bf16[128,256]{1,0:T(8,128)(2,1)S(1)}, bf16[128,256]{1,0:T(8,128)(2,1)}, u32[]{:S(2)}) copy-start(bf16[128,256]{1,0:T(8,128)(2,1)} %points_ref.1) | copy-start | bytes 196612
  1.0 3.8 %collective-permute-start = (bf16[128,256]{1,0:T(8,128)(2,1)S(1)}, bf16[128,256]{1,0:T(8,128)(2,1)S(1)}, u32[]{:S(2)}, u32[]{:S(2)}) collective-permute-start(bf16[128,256]{1,0:T(8,128)(2,1)S(1)} %tangent.1.tangent_ref), channel_id=1, source_target_pairs={{0,8},{4,12},{8,0},{12,4},{16,24},{20,28},{24,16},{28,20},{32,40},... | collective-permute-start | bytes 196616 | tf_op jit(solution)/shard_map/ppermute | solution.py:354
  4.8 30.2 %copy-start.9 = (s32[1,1,64]{2,1,0:T(1,128)S(1)}, s32[1,1,64]{2,1,0:T(1,128)}, u32[]{:S(2)}) copy-start(s32[1,1,64]{2,1,0:T(1,128)} %param.16) | copy-start | bytes 772
  4.8 4.0 %collective-permute-start.1 = (bf16[256,256]{1,0:T(8,128)(2,1)S(1)}, bf16[256,256]{1,0:T(8,128)(2,1)S(1)}, u32[]{:S(2)}, u32[]{:S(2)}) collective-permute-start(bf16[256,256]{1,0:T(8,128)(2,1)S(1)} %pad_maximum_fusion.3), channel_id=1, source_target_pairs={{0,32},{4,36},{8,40},{12,44},{16,48},{20,52},{24,56},{28,60},{32,0... | collective-permute-start | bytes 393224 | tf_op jit(solution)/shard_map/ppermute | solution.py:354
  6.4 24.7 %collective-permute-start.6 = (bf16[128,256]{1,0:T(8,128)(2,1)S(1)}, bf16[128,256]{1,0:T(8,128)(2,1)S(1)}, u32[]{:S(2)}, u32[]{:S(2)}) collective-permute-start(bf16[128,256]{1,0:T(8,128)(2,1)S(1)} %tangent.1.tangent_ref), channel_id=1, source_target_pairs={{0,1},{1,0},{2,3},{3,2},{4,5},{5,4},{6,7},{7,6},{8,9},{9,8},{10,11... | collective-permute-start | bytes 196616 | tf_op jit(solution)/shard_map/ppermute | solution.py:354
  8.8 5.6 %collective-permute-start.4 = (bf16[256,256]{1,0:T(8,128)(2,1)S(1)}, bf16[256,256]{1,0:T(8,128)(2,1)S(1)}, u32[]{:S(2)}, u32[]{:S(2)}) collective-permute-start(bf16[256,256]{1,0:T(8,128)(2,1)S(1)} %get-tuple-element.22), channel_id=1, source_target_pairs={{0,96},{4,100},{8,104},{12,108},{16,112},{20,116},{24,120},{28,124... | collective-permute-start | bytes 393224 | tf_op jit(solution)/shard_map/ppermute | solution.py:354
  11.8 5.4 %collective-permute-start.2 = (bf16[256,256]{1,0:T(8,128)(2,1)S(1)}, bf16[256,256]{1,0:T(8,128)(2,1)S(1)}, u32[]{:S(2)}, u32[]{:S(2)}) collective-permute-start(bf16[256,256]{1,0:T(8,128)(2,1)S(1)} %get-tuple-element.21), channel_id=1, source_target_pairs={{0,24},{4,28},{8,16},{12,20},{16,8},{20,12},{24,0},{28,4},{32,56},... | collective-permute-start | bytes 393224 | tf_op jit(solution)/shard_map/ppermute | solution.py:354
  14.4 8.3 %collective-permute-start.5 = (bf16[512,256]{1,0:T(8,128)(2,1)S(1)}, bf16[512,256]{1,0:T(8,128)(2,1)S(1)}, u32[]{:S(2)}, u32[]{:S(2)}) collective-permute-start(bf16[512,256]{1,0:T(8,128)(2,1)S(1)} %pad_maximum_fusion.1), channel_id=1, source_target_pairs={{0,24},{4,28},{8,16},{12,20},{16,8},{20,12},{24,0},{28,4},{32,56},... | collective-permute-start | bytes 786440 | tf_op jit(solution)/shard_map/ppermute | solution.py:354
  17.2 8.7 %collective-permute-start.3 = (bf16[512,256]{1,0:T(8,128)(2,1)S(1)}, bf16[512,256]{1,0:T(8,128)(2,1)S(1)}, u32[]{:S(2)}, u32[]{:S(2)}) collective-permute-start(bf16[512,256]{1,0:T(8,128)(2,1)S(1)} %pad_maximum_fusion), channel_id=1, source_target_pairs={{0,96},{4,100},{8,104},{12,108},{16,112},{20,116},{24,120},{28,124... | collective-permute-start | bytes 786440 | tf_op jit(solution)/shard_map/ppermute | solution.py:354
  22.7 19.8 %collective-permute-start.9 = (bf16[1024,256]{1,0:T(8,128)(2,1)S(1)}, bf16[1024,256]{1,0:T(8,128)(2,1)S(1)}, u32[]{:S(2)}, u32[]{:S(2)}) collective-permute-start(bf16[1024,256]{1,0:T(8,128)(2,1)S(1)} %constant_dynamic-update-slice_fusion.3.second_ref), channel_id=1, source_target_pairs={{0,4},{4,0},{8,12},{12,8},{16,20},{20,16},{24,28},{28,24},{32,36},... | collective-permute-start | bytes 1572872 | tf_op jit(solution)/shard_map/ppermute | solution.py:354
  26.0 16.6 %collective-permute-start.8 = (bf16[1024,256]{1,0:T(8,128)(2,1)S(1)}, bf16[1024,256]{1,0:T(8,128)(2,1)S(1)}, u32[]{:S(2)}, u32[]{:S(2)}) collective-permute-start(bf16[1024,256]{1,0:T(8,128)(2,1)S(1)} %constant_dynamic-update-slice_fusion.first_ref), channel_id=1, source_target_pairs={{0,4},{4,0},{8,12},{12,8},{16,20},{20,16},{24,28},{28,24},{32,36},... | collective-permute-start | bytes 1572872 | tf_op jit(solution)/shard_map/ppermute | solution.py:354
  31.2 10.2 %collective-permute-start.7 = (bf16[256,256]{1,0:T(8,128)(2,1)S(1)}, bf16[256,256]{1,0:T(8,128)(2,1)S(1)}, u32[]{:S(2)}, u32[]{:S(2)}) collective-permute-start(bf16[256,256]{1,0:T(8,128)(2,1)S(1)} %pad_maximum_fusion.7), channel_id=1, source_target_pairs={{0,3},{1,2},{2,1},{3,0},{4,7},{5,6},{6,5},{7,4},{8,11},{9,10},{10,... | collective-permute-start | bytes 393224 | tf_op jit(solution)/shard_map/ppermute | solution.py:354
  35.6 5.8 %copy-start.1 = (bf16[256,256]{1,0:T(8,128)(2,1)S(1)}, bf16[256,256]{1,0:T(8,128)(2,1)}, u32[]{:S(2)}) copy-start(bf16[256,256]{1,0:T(8,128)(2,1)} %wk_ref.3) | copy-start | bytes 393220
  35.6 5.8 %copy-start.7 = (bf16[256,256]{1,0:T(8,128)(2,1)S(1)}, bf16[256,256]{1,0:T(8,128)(2,1)}, u32[]{:S(2)}) copy-start(bf16[256,256]{1,0:T(8,128)(2,1)} %wq_ref.1) | copy-start | bytes 393220
  35.6 5.8 %copy-start.8 = (bf16[256,256]{1,0:T(8,128)(2,1)S(1)}, bf16[256,256]{1,0:T(8,128)(2,1)}, u32[]{:S(2)}) copy-start(bf16[256,256]{1,0:T(8,128)(2,1)} %wv_ref.1) | copy-start | bytes 393220
  42.5 1.6 %copy-start = (bf16[65,128,128]{2,1,0:T(8,128)(2,1)S(1)}, bf16[65,128,128]{2,1,0:T(8,128)(2,1)}, u32[]{:S(2)}) copy-start(bf16[65,128,128]{2,1,0:T(8,128)(2,1)} %get-tuple-element.20.bias_ref) | copy-start | bytes 6389764
  42.5 1.6 %copy-start.4 = (s32[168]{0:T(256)S(1)}, s32[168]{0:T(256)}, u32[]{:S(2)}) copy-start(s32[168]{0:T(256)} %get-tuple-element.18.tile_list) | copy-start | bytes 2020
  42.5 1.6 %copy-start.5 = (s32[4]{0:T(128)S(1)}, s32[4]{0:T(128)}, u32[]{:S(2)}) copy-start(s32[4]{0:T(128)} %get-tuple-element.19.counts) | copy-start | bytes 52
  52.4 7.2 %copy-start.2 = (bf16[256,256]{1,0:T(8,128)(2,1)S(1)}, bf16[256,256]{1,0:T(8,128)(2,1)}, u32[]{:S(2)}) copy-start(bf16[256,256]{1,0:T(8,128)(2,1)} %wo_ref.1) | copy-start | bytes 393220
  52.5 7.2 %copy-start.6 = (f32[256]{0:T(256)S(1)}, f32[256]{0:T(256)}, u32[]{:S(2)}) copy-start(f32[256]{0:T(256)} %param.14) | copy-start | bytes 3076
  52.5 6.0 %collective-permute-start.12 = (bf16[288,128]{1,0:T(8,128)(2,1)S(1)}, bf16[288,128]{1,0:T(8,128)(2,1)S(1)}, u32[]{:S(2)}, u32[]{:S(2)}) collective-permute-start(bf16[288,128]{1,0:T(8,128)(2,1)S(1)} %shard_map.93), channel_id=1, source_target_pairs={{0,1},{1,0},{2,3},{3,2},{4,5},{5,4},{6,7},{7,6},{8,9},{9,8},{10,11... | collective-permute-start | bytes 221192 | tf_op jit(solution)/shard_map/ppermute | solution.py:354
  52.6 7.1 %collective-permute-start.11 = (bf16[288,128]{1,0:T(8,128)(2,1)S(1)}, bf16[288,128]{1,0:T(8,128)(2,1)S(1)}, u32[]{:S(2)}, u32[]{:S(2)}) collective-permute-start(bf16[288,128]{1,0:T(8,128)(2,1)S(1)} %shard_map.92), channel_id=1, source_target_pairs={{0,3},{1,2},{2,1},{3,0},{4,7},{5,6},{6,5},{7,4},{8,11},{9,10},{10,... | collective-permute-start | bytes 221192 | tf_op jit(solution)/shard_map/ppermute | solution.py:354
  52.7 7.0 %collective-permute-start.10 = (bf16[288,128]{1,0:T(8,128)(2,1)S(1)}, bf16[288,128]{1,0:T(8,128)(2,1)S(1)}, u32[]{:S(2)}, u32[]{:S(2)}) collective-permute-start(bf16[288,128]{1,0:T(8,128)(2,1)S(1)} %shard_map.91), channel_id=1, source_target_pairs={{0,2},{1,3},{2,0},{3,1},{4,6},{5,7},{6,4},{7,5},{8,10},{9,11},{10,... | collective-permute-start | bytes 221192 | tf_op jit(solution)/shard_map/ppermute | solution.py:354
